TPU v7x, 32 devices: a whole 2x2x4 slice. The times are simulated.
32 devices in a mesh: det: 4 (over y, x), obs: 8 (over z, core).
Axes of the slice: x: 2, y: 2, z: 4, core: 2. Of those that a mesh axis runs over, the one named last changes fastest.
Arguments:
- tod: float32 [4, 8, 8192], P('det', 'obs'), may hold values from -200 to 200
- angle: float32 [4, 8, 8192], P('det', 'obs'), may hold values from -3.140625 to 3.140625
- pix_in: int32 [4, 8, 8192], P('det', 'obs'), may hold values from 0 to 63
- tile_block: int32 [4, 8, 32], P('det', 'obs'), may hold values from 0 to 511
- base_len: int32 [4, 8, 40], P('det', 'obs'), may hold values from 1 to 384, 8192 in all within a row
- touched: int32 [8, 16], P('obs'), may hold values from 0 to 511, as said below
Outputs:
- baselines: float32 [4, 8, 40], P('det', 'obs')
- residual_rate: float32 [4, 8, 40], P('det', 'obs')
Inputs may be any that keep to these rules, and one draw needn't show every extreme that they name: `touched`: each row lists 16 distinct patches; patch p is held by owner p // 64; at most 4 patches of one row share an owner, and one owner holds exactly 4 patches of every row.
All inputs are finite; a program needn't handle non-finite values.
Results may differ from a plain program's by a relative error of at most 0.0003.
Values sent between devices are 32-bit elements; how exact they have to be, the bound alone decides.
A program may use at most 128 MiB of HBM per device.

v0:
```python
import math
import jax
import jax.numpy as jnp
from jax import lax
from jax.sharding import PartitionSpec as P

TILE = 256
BLK = 64
PATCH_PIX = 2048
PT = 16
PATCH_OWN = 64
ITERS = 2
UPPER_LIMIT = lax.Precision.HIGHEST


def pixel_inverse(hits):
    a11 = hits[:, 0] + 1.0
    a12 = hits[:, 1]
    a13 = hits[:, 2]
    a22 = hits[:, 3] + 1.0
    a23 = hits[:, 4]
    a33 = hits[:, 5] + 1.0
    c11 = a22 * a33 - a23 * a23
    c12 = a13 * a23 - a12 * a33
    c13 = a12 * a23 - a13 * a22
    c22 = a11 * a33 - a13 * a13
    c23 = a12 * a13 - a11 * a23
    c33 = a11 * a22 - a12 * a12
    determinant = a11 * c11 + a12 * c12 + a13 * c13
    return jnp.stack([c11, c12, c13, c22, c23, c33], axis=1) / determinant[:, None]


def apply_inverse(inverse, pixel_binned_map):
    first = (
        inverse[:, 0] * pixel_binned_map[:, 0]
        + inverse[:, 1] * pixel_binned_map[:, 1]
        + inverse[:, 2] * pixel_binned_map[:, 2]
    )
    second = (
        inverse[:, 1] * pixel_binned_map[:, 0]
        + inverse[:, 3] * pixel_binned_map[:, 1]
        + inverse[:, 4] * pixel_binned_map[:, 2]
    )
    third = (
        inverse[:, 2] * pixel_binned_map[:, 0]
        + inverse[:, 4] * pixel_binned_map[:, 1]
        + inverse[:, 5] * pixel_binned_map[:, 2]
    )
    return jnp.stack([first, second, third], axis=1)


def combine_det(partial_value):
    total = lax.psum(partial_value, "det")
    return total


def squares(residual_vector):
    return lax.psum(jnp.sum(residual_vector * residual_vector), ("det", "obs"))


def body(tod, angle, pix_in, tile_block, base_len, touched):
    signal = tod[0, 0]
    inner = pix_in[0, 0]
    tile_rows = tile_block[0, 0]
    lengths = base_len[0, 0]
    patch_list = touched[0]
    samples = signal.shape[0]
    nbase = lengths.shape[0]
    ntile = samples // TILE
    group = math.gcd(ntile, 64)
    groups = ntile // group
    blocks = PATCH_PIX // BLK
    local_blocks = PT * blocks
    obs_count = lax.axis_size("obs")
    cap = max(2, 2 * PT // obs_count)
    slots = obs_count * cap
    cos_w = jnp.cos(2.0 * angle[0, 0])
    sin_w = jnp.sin(2.0 * angle[0, 0])
    ends = jnp.cumsum(lengths)
    base_index = jnp.searchsorted(ends, jnp.arange(samples, dtype=jnp.int32), side="right")
    inner_groups = inner.reshape(groups, group, TILE)
    cos_groups = cos_w.reshape(groups, group, TILE)
    sin_groups = sin_w.reshape(groups, group, TILE)
    pixel_iota = jnp.arange(BLK, dtype=jnp.int32)
    tile_select = (tile_rows[None, :] == jnp.arange(local_blocks, dtype=jnp.int32)[:, None]).astype(
        jnp.float32
    )

    def tile_indicator_matrix(index):
        return (index[:, None, :] == pixel_iota[None, :, None]).astype(jnp.float32)

    def bin_local(value_entries):
        comps = value_entries.shape[0]
        grouped = value_entries.reshape(comps, groups, group, TILE).transpose(1, 2, 0, 3)

        def bin_one_group(index_couple):
            return jnp.einsum(
                "awv,agv->awg",
                index_couple[0],
                tile_indicator_matrix(index_couple[1]),
                precision=UPPER_LIMIT,
            )

        per_tile = lax.map(bin_one_group, (grouped, inner_groups)).reshape(ntile, comps * BLK)
        summed = jnp.dot(tile_select, per_tile, precision=UPPER_LIMIT)
        return (
            summed.reshape(PT, blocks, comps, BLK)
            .transpose(0, 2, 1, 3)
            .reshape(PT, comps, PATCH_PIX)
        )

    def unbin_local(local_map):
        rows = (
            local_map.reshape(PT, 3, blocks, BLK)
            .transpose(0, 2, 1, 3)
            .reshape(local_blocks, 3 * BLK)
        )
        picked = jnp.take(rows, tile_rows, axis=0).reshape(groups, group, 3, BLK)

        def unbin_one_group(partition_pieces):
            value_entries = jnp.einsum(
                "jwx,jxd->jwd",
                partition_pieces[0],
                tile_indicator_matrix(partition_pieces[1]),
                precision=UPPER_LIMIT,
            )
            return (
                value_entries[:, 0]
                + partition_pieces[2] * value_entries[:, 1]
                + partition_pieces[3] * value_entries[:, 2]
            )

        return lax.map(unbin_one_group, (picked, inner_groups, cos_groups, sin_groups)).reshape(
            samples
        )

    owner_of = patch_list // PATCH_OWN
    slot_of = patch_list % PATCH_OWN
    positions = jnp.arange(PT, dtype=jnp.int32)
    before = (owner_of[None, :] == owner_of[:, None]) & (positions[None, :] < positions[:, None])
    rank = jnp.sum(before.astype(jnp.int32), axis=1)
    target = owner_of * cap + rank
    placed = target[None, :] == jnp.arange(slots, dtype=jnp.int32)[:, None]
    packing = placed.astype(jnp.float32)
    send_ids = (jnp.sum(jnp.where(placed, slot_of[None, :] + 1, 0), axis=1) - 1).reshape(
        obs_count, cap
    )

    def pack_map(total):
        comps, width = (total.shape[1], total.shape[2])
        return jnp.dot(packing, total.reshape(PT, comps * width), precision=UPPER_LIMIT).reshape(
            obs_count, cap, comps, width
        )

    def unpack_map(returned):
        width = returned.shape[3]
        return jnp.dot(
            packing.T, returned.reshape(slots, 3 * width), precision=UPPER_LIMIT
        ).reshape(PT, 3, width)

    ones = jnp.ones_like(signal)
    first_values = jnp.stack(
        [
            signal,
            signal * cos_w,
            signal * sin_w,
            ones,
            cos_w,
            sin_w,
            cos_w * cos_w,
            cos_w * sin_w,
            sin_w * sin_w,
        ]
    )
    first_total = combine_det(bin_local(first_values))
    received, source_ids = (
        lax.all_to_all(pack_map(first_total), "obs", split_axis=0, concat_axis=0, tiled=True),
        lax.all_to_all(send_ids, "obs", split_axis=0, concat_axis=0, tiled=True),
    )
    owner_pick = (
        source_ids.reshape(slots)[None, :] == jnp.arange(PATCH_OWN, dtype=jnp.int32)[:, None]
    ).astype(jnp.float32)

    def gather_owner(arrived):
        comps, width = (arrived.shape[2], arrived.shape[3])
        return jnp.dot(
            owner_pick, arrived.reshape(slots, comps * width), precision=UPPER_LIMIT
        ).reshape(PATCH_OWN, comps, width)

    def return_map(owned):
        width = owned.shape[2]
        outgoing = jnp.dot(
            owner_pick.T, owned.reshape(PATCH_OWN, 3 * width), precision=UPPER_LIMIT
        ).reshape(obs_count, cap, 3, width)
        return lax.all_to_all(outgoing, "obs", split_axis=0, concat_axis=0, tiled=True)

    accumulated = gather_owner(received)
    inverse = pixel_inverse(accumulated[:, 3:])
    start_map = apply_inverse(inverse, accumulated[:, :3])
    start_local = unpack_map(return_map(start_map))
    cleaned = signal - unbin_local(start_local)
    right_side = jax.ops.segment_sum(
        cleaned, base_index, num_segments=nbase, indices_are_sorted=True
    )
    solution = jnp.zeros_like(right_side)
    residual_vector = right_side
    direction = right_side
    norm_now = squares(residual_vector)
    for step in range(ITERS):
        expanded = jnp.take(direction, base_index)
        apply_value_entries = jnp.stack([expanded, expanded * cos_w, expanded * sin_w])
        apply_total = combine_det(bin_local(apply_value_entries))
        apply_arrived = lax.all_to_all(
            pack_map(apply_total), "obs", split_axis=0, concat_axis=0, tiled=True
        )
        solved = apply_inverse(inverse, gather_owner(apply_arrived))
        apply_local_map = unpack_map(return_map(solved))
        image = jax.ops.segment_sum(
            expanded - unbin_local(apply_local_map),
            base_index,
            num_segments=nbase,
            indices_are_sorted=True,
        )
        alpha = norm_now / lax.psum(jnp.sum(direction * image), ("det", "obs"))
        solution = solution + alpha * direction
        residual_vector = residual_vector - alpha * image
        if step + 1 < ITERS:
            norm_next = squares(residual_vector)
            direction = residual_vector + norm_next / norm_now * direction
            norm_now = norm_next
    rate = residual_vector / lengths.astype(jnp.float32)
    return (solution[None, None], rate[None, None])


def solution(mesh):
    placed = (
        P("det", "obs", None),
        P("det", "obs", None),
        P("det", "obs", None),
        P("det", "obs", None),
        P("det", "obs", None),
        P("obs", None),
    )
    return jax.shard_map(
        body,
        mesh=mesh,
        in_specs=placed,
        out_specs=(P("det", "obs", None), P("det", "obs", None)),
        check_vma=False,
    )
```

profile of v0, /device:TPU:12, one launch (start us, length us, event | category | flops | bytes accessed | tf_op | source)
XLA Modules:
  0.0 1070.5 jit_solution(13468639081524979222)
XLA Ops:
  18.3 5.3 all-to-all-start
  23.7 49.2 %all-reduce.5.cloned.1.call-done = f32[9,2048,16]{1,2,0:T(8,128)} async-done(((f32[9,2048,16]{1,2,0:T(8,128)}), f32[9,2048,16]{1,2,0:T(8,128)}) %all-reduce.5.cloned.1.call-update) | async-done | bytes 1179664 | tf_op jit(solution)/shard_map/psum | solution.py:53
  77.3 5.8 all-to-all-start.1
  84.3 50.0 %all-to-all-done.1 = f32[8,4,9,2048]{3,1,2,0:T(4,128)S(1)} async-done(((f32[8,4,9,2048]{3,1,2,0:T(4,128)}), f32[8,4,9,2048]{3,1,2,0:T(4,128)S(1)}, u32[]{:S(2)}, u32[]{:S(2)}) %all-to-all-start.1) | async-done | bytes 2359328 | tf_op jit(solution)/shard_map/all_to_all | solution.py:177
  142.9 7.5 all-to-all-start.2
  150.6 312.5 %while.24 = (s32[]{:T(128)}, u32[8192]{0:T(1024)S(1)}, u32[8192]{0:T(1024)S(1)}, s32[40]{0:T(128)S(1)}, s32[]{:T(128)}, /*index=5*/s32[]{:T(128)}) while((s32[]{:T(128)}, u32[8192]{0:T(1024)S(1)}, u32[8192]{0:T(1024)S(1)}, s32[40]{0:T(128)S(1)}, s32[]{:T(128)}, /*index=5*/s32[]{:T(128)}) %tuple.233), condition=%wide.region_2.3_spmd.clone, body=%wide.region_1.2_spmd.clone.sunk | while | flops 1392643 | bytes 262864 | solution.py:80
  152.8 25.0 %fusion.141 = u32[8192]{0:T(1024)S(1)} fusion(u32[8192]{0:T(1024)S(1)} %get-tuple-element.525, u32[8192]{0:T(1024)S(1)} %get-tuple-element.524, s32[]{:T(128)} %bitcast.438, s32[]{:T(128)} %bitcast.439, s32[]{:T(128)} %bitcast.440, s32[]{:T(128)} %bitcast.441, s32[]{:T(128)} %bitcast.442, s32[]{:T(128)} %bitcast.443, s32[]{:T(128)} %bitcast.444, ...), kind=kLoop, calls=%fused_computation.8.clone.1 | loop fusion | flops 696320 | bytes 98465 | tf_op jit(solution)/shard_map/jit(searchsorted)/jit(_searchsorted_scan_impl)/vmap(jit(_searchsorted_scan_impl))/while/body/eval_jaxpr/select_n | solution.py:80
  177.7 25.0 %fusion.140 = u32[8192]{0:T(1024)S(1)} fusion(u32[8192]{0:T(1024)S(1)} %get-tuple-element.525, u32[8192]{0:T(1024)S(1)} %get-tuple-element.524, s32[]{:T(128)} %bitcast.438, s32[]{:T(128)} %bitcast.439, s32[]{:T(128)} %bitcast.440, s32[]{:T(128)} %bitcast.441, s32[]{:T(128)} %bitcast.442, s32[]{:T(128)} %bitcast.443, s32[]{:T(128)} %bitcast.444, ...), kind=kLoop, calls=%fused_computation.9.clone.1 | loop fusion | flops 696320 | bytes 98465 | tf_op jit(solution)/shard_map/jit(searchsorted)/jit(_searchsorted_scan_impl)/vmap(jit(_searchsorted_scan_impl))/while/body/eval_jaxpr/select_n | solution.py:80
  204.9 25.0 %fusion.141 = u32[8192]{0:T(1024)S(1)} fusion(u32[8192]{0:T(1024)S(1)} %get-tuple-element.525, u32[8192]{0:T(1024)S(1)} %get-tuple-element.524, s32[]{:T(128)} %bitcast.438, s32[]{:T(128)} %bitcast.439, s32[]{:T(128)} %bitcast.440, s32[]{:T(128)} %bitcast.441, s32[]{:T(128)} %bitcast.442, s32[]{:T(128)} %bitcast.443, s32[]{:T(128)} %bitcast.444, ...), kind=kLoop, calls=%fused_computation.8.clone.1 | loop fusion | flops 696320 | bytes 98465 | tf_op jit(solution)/shard_map/jit(searchsorted)/jit(_searchsorted_scan_impl)/vmap(jit(_searchsorted_scan_impl))/while/body/eval_jaxpr/select_n | solution.py:80
  229.8 25.0 %fusion.140 = u32[8192]{0:T(1024)S(1)} fusion(u32[8192]{0:T(1024)S(1)} %get-tuple-element.525, u32[8192]{0:T(1024)S(1)} %get-tuple-element.524, s32[]{:T(128)} %bitcast.438, s32[]{:T(128)} %bitcast.439, s32[]{:T(128)} %bitcast.440, s32[]{:T(128)} %bitcast.441, s32[]{:T(128)} %bitcast.442, s32[]{:T(128)} %bitcast.443, s32[]{:T(128)} %bitcast.444, ...), kind=kLoop, calls=%fused_computation.9.clone.1 | loop fusion | flops 696320 | bytes 98465 | tf_op jit(solution)/shard_map/jit(searchsorted)/jit(_searchsorted_scan_impl)/vmap(jit(_searchsorted_scan_impl))/while/body/eval_jaxpr/select_n | solution.py:80
  256.9 25.0 %fusion.141 = u32[8192]{0:T(1024)S(1)} fusion(u32[8192]{0:T(1024)S(1)} %get-tuple-element.525, u32[8192]{0:T(1024)S(1)} %get-tuple-element.524, s32[]{:T(128)} %bitcast.438, s32[]{:T(128)} %bitcast.439, s32[]{:T(128)} %bitcast.440, s32[]{:T(128)} %bitcast.441, s32[]{:T(128)} %bitcast.442, s32[]{:T(128)} %bitcast.443, s32[]{:T(128)} %bitcast.444, ...), kind=kLoop, calls=%fused_computation.8.clone.1 | loop fusion | flops 696320 | bytes 98465 | tf_op jit(solution)/shard_map/jit(searchsorted)/jit(_searchsorted_scan_impl)/vmap(jit(_searchsorted_scan_impl))/while/body/eval_jaxpr/select_n | solution.py:80
  281.9 25.0 %fusion.140 = u32[8192]{0:T(1024)S(1)} fusion(u32[8192]{0:T(1024)S(1)} %get-tuple-element.525, u32[8192]{0:T(1024)S(1)} %get-tuple-element.524, s32[]{:T(128)} %bitcast.438, s32[]{:T(128)} %bitcast.439, s32[]{:T(128)} %bitcast.440, s32[]{:T(128)} %bitcast.441, s32[]{:T(128)} %bitcast.442, s32[]{:T(128)} %bitcast.443, s32[]{:T(128)} %bitcast.444, ...), kind=kLoop, calls=%fused_computation.9.clone.1 | loop fusion | flops 696320 | bytes 98465 | tf_op jit(solution)/shard_map/jit(searchsorted)/jit(_searchsorted_scan_impl)/vmap(jit(_searchsorted_scan_impl))/while/body/eval_jaxpr/select_n | solution.py:80
  309.0 25.0 %fusion.141 = u32[8192]{0:T(1024)S(1)} fusion(u32[8192]{0:T(1024)S(1)} %get-tuple-element.525, u32[8192]{0:T(1024)S(1)} %get-tuple-element.524, s32[]{:T(128)} %bitcast.438, s32[]{:T(128)} %bitcast.439, s32[]{:T(128)} %bitcast.440, s32[]{:T(128)} %bitcast.441, s32[]{:T(128)} %bitcast.442, s32[]{:T(128)} %bitcast.443, s32[]{:T(128)} %bitcast.444, ...), kind=kLoop, calls=%fused_computation.8.clone.1 | loop fusion | flops 696320 | bytes 98465 | tf_op jit(solution)/shard_map/jit(searchsorted)/jit(_searchsorted_scan_impl)/vmap(jit(_searchsorted_scan_impl))/while/body/eval_jaxpr/select_n | solution.py:80
  334.0 25.0 %fusion.140 = u32[8192]{0:T(1024)S(1)} fusion(u32[8192]{0:T(1024)S(1)} %get-tuple-element.525, u32[8192]{0:T(1024)S(1)} %get-tuple-element.524, s32[]{:T(128)} %bitcast.438, s32[]{:T(128)} %bitcast.439, s32[]{:T(128)} %bitcast.440, s32[]{:T(128)} %bitcast.441, s32[]{:T(128)} %bitcast.442, s32[]{:T(128)} %bitcast.443, s32[]{:T(128)} %bitcast.444, ...), kind=kLoop, calls=%fused_computation.9.clone.1 | loop fusion | flops 696320 | bytes 98465 | tf_op jit(solution)/shard_map/jit(searchsorted)/jit(_searchsorted_scan_impl)/vmap(jit(_searchsorted_scan_impl))/while/body/eval_jaxpr/select_n | solution.py:80
  361.1 25.0 %fusion.141 = u32[8192]{0:T(1024)S(1)} fusion(u32[8192]{0:T(1024)S(1)} %get-tuple-element.525, u32[8192]{0:T(1024)S(1)} %get-tuple-element.524, s32[]{:T(128)} %bitcast.438, s32[]{:T(128)} %bitcast.439, s32[]{:T(128)} %bitcast.440, s32[]{:T(128)} %bitcast.441, s32[]{:T(128)} %bitcast.442, s32[]{:T(128)} %bitcast.443, s32[]{:T(128)} %bitcast.444, ...), kind=kLoop, calls=%fused_computation.8.clone.1 | loop fusion | flops 696320 | bytes 98465 | tf_op jit(solution)/shard_map/jit(searchsorted)/jit(_searchsorted_scan_impl)/vmap(jit(_searchsorted_scan_impl))/while/body/eval_jaxpr/select_n | solution.py:80
  386.1 25.0 %fusion.140 = u32[8192]{0:T(1024)S(1)} fusion(u32[8192]{0:T(1024)S(1)} %get-tuple-element.525, u32[8192]{0:T(1024)S(1)} %get-tuple-element.524, s32[]{:T(128)} %bitcast.438, s32[]{:T(128)} %bitcast.439, s32[]{:T(128)} %bitcast.440, s32[]{:T(128)} %bitcast.441, s32[]{:T(128)} %bitcast.442, s32[]{:T(128)} %bitcast.443, s32[]{:T(128)} %bitcast.444, ...), kind=kLoop, calls=%fused_computation.9.clone.1 | loop fusion | flops 696320 | bytes 98465 | tf_op jit(solution)/shard_map/jit(searchsorted)/jit(_searchsorted_scan_impl)/vmap(jit(_searchsorted_scan_impl))/while/body/eval_jaxpr/select_n | solution.py:80
  413.2 25.0 %fusion.141 = u32[8192]{0:T(1024)S(1)} fusion(u32[8192]{0:T(1024)S(1)} %get-tuple-element.525, u32[8192]{0:T(1024)S(1)} %get-tuple-element.524, s32[]{:T(128)} %bitcast.438, s32[]{:T(128)} %bitcast.439, s32[]{:T(128)} %bitcast.440, s32[]{:T(128)} %bitcast.441, s32[]{:T(128)} %bitcast.442, s32[]{:T(128)} %bitcast.443, s32[]{:T(128)} %bitcast.444, ...), kind=kLoop, calls=%fused_computation.8.clone.1 | loop fusion | flops 696320 | bytes 98465 | tf_op jit(solution)/shard_map/jit(searchsorted)/jit(_searchsorted_scan_impl)/vmap(jit(_searchsorted_scan_impl))/while/body/eval_jaxpr/select_n | solution.py:80
  438.2 25.0 %fusion.140 = u32[8192]{0:T(1024)S(1)} fusion(u32[8192]{0:T(1024)S(1)} %get-tuple-element.525, u32[8192]{0:T(1024)S(1)} %get-tuple-element.524, s32[]{:T(128)} %bitcast.438, s32[]{:T(128)} %bitcast.439, s32[]{:T(128)} %bitcast.440, s32[]{:T(128)} %bitcast.441, s32[]{:T(128)} %bitcast.442, s32[]{:T(128)} %bitcast.443, s32[]{:T(128)} %bitcast.444, ...), kind=kLoop, calls=%fused_computation.9.clone.1 | loop fusion | flops 696320 | bytes 98465 | tf_op jit(solution)/shard_map/jit(searchsorted)/jit(_searchsorted_scan_impl)/vmap(jit(_searchsorted_scan_impl))/while/body/eval_jaxpr/select_n | solution.py:80
  479.4 57.2 %scatter_custom_fusion = f32[40]{0:T(128)S(1)} fusion(s32[8192]{0:T(1024)} %convert_element_type.34, f32[8192]{0:T(1024)S(1)} %add_subtract_fusion.2, f32[]{:T(128)} %constant.148.clone.1), kind=kCustom, calls=%fused_computation.230 | custom fusion | flops 8192 | bytes 672 | tf_op jit(solution)/shard_map/scatter-add | solution.py:202
  538.6 25.7 %fusion.114 = (f32[8192]{0:T(1024)S(1)}, f32[8192]{0:T(1024)S(1)}, pred[8192]{0:T(1024)(128)(4,1)S(1)}, pred[8192]{0:T(1024)(128)(4,1)S(1)}, pred[8192]{0:T(1024...) fusion(f32[8192]{0:T(1024)S(1)} %bitcast.499, ...), kind=kLoop, calls=%fused_computation.235 | loop fusion | flops 712704 | bytes 458912 | tf_op jit(solution)/shard_map/mul | solution.py:211
  571.7 44.1 %all-reduce.7.cloned.1.call-done = f32[3,2048,16]{1,2,0:T(8,128)} async-done(((f32[3,2048,16]{1,2,0:T(8,128)}), f32[3,2048,16]{1,2,0:T(8,128)}) %all-reduce.7.cloned.1.call-update) | async-done | bytes 393232 | tf_op jit(solution)/shard_map/psum | solution.py:53
  617.4 23.8 %all_to_all.36 = f32[8,4,3,2048]{3,1,2,0:T(4,128)S(1)} all-to-all(f32[8,4,3,2048]{3,1,2,0:T(4,128)S(1)} %fusion.51), channel_id=1, replica_groups=mesh['det'=4,'obs'=8] {'obs'}, dimensions={0} | all-to-all | bytes 1572864 | tf_op jit(solution)/shard_map/all_to_all | solution.py:213
  644.5 23.4 %all_to_all.37 = f32[8,4,3,2048]{3,1,2,0:T(4,128)S(1)} all-to-all(f32[8,4,3,2048]{3,1,2,0:T(4,128)S(1)} %fusion.15), channel_id=1, replica_groups=mesh['det'=4,'obs'=8] {'obs'}, dimensions={0} | all-to-all | bytes 1572864 | tf_op jit(solution)/shard_map/all_to_all | solution.py:195
  682.4 57.2 %scatter_custom_fusion.1 = f32[40]{0:T(128)S(1)} fusion(s32[8192]{0:T(1024)} %convert_element_type.34, f32[8192]{0:T(1024)S(1)} %add_subtract_fusion.1, f32[]{:T(128)} %constant.148.clone.1), kind=kCustom, calls=%fused_computation.228 | custom fusion | flops 8192 | bytes 672 | tf_op jit(solution)/shard_map/scatter-add | solution.py:218
  740.1 41.3 %all-reduce = (f32[]{:T(128)}, f32[]{:T(128)}) all-reduce(f32[]{:T(128)} %get-tuple-element.196, f32[]{:T(128)} %get-tuple-element.195), channel_id=1, replica_groups=mesh['det'=4,'obs'=8] {'det','obs'}, use_global_device_ids=true, to_apply=%region_8.10 | all-reduce | flops 2 | bytes 16 | tf_op jit(solution)/shard_map/psum | solution.py:58
  783.4 39.9 %psum.53 = f32[]{:T(128)} all-reduce(f32[]{:T(128)} %get-tuple-element.209), channel_id=1, replica_groups=mesh['det'=4,'obs'=8] {'det','obs'}, use_global_device_ids=true, to_apply=%region_14.17 | all-reduce | flops 1 | bytes 8 | tf_op jit(solution)/shard_map/psum | solution.py:58
  826.7 25.8 %fusion.113 = (f32[8192]{0:T(1024)S(1)}, f32[8192]{0:T(1024)S(1)}) fusion(f32[8192]{0:T(1024)S(1)} %bitcast.501, pred[8192]{0:T(1024)(128)(4,1)} %get-tuple-element.252, pred[8192]{0:T(1024)(128)(4,1)} %get-tuple-element.251, pred[8192]{0:T(1024)(128)(4,1)} %get-tuple-element.250, pred[8192]{0:T(1024)(128)(4,1)} %get-tuple-element.249, ...), kind=kLoop, calls=%fused_computation.234 | loop fusion | flops 335872 | bytes 426144 | tf_op jit(solution)/shard_map/mul | solution.py:211
  859.8 44.0 %all-reduce.9.cloned.1.call-done = f32[3,2048,16]{1,2,0:T(8,128)} async-done(((f32[3,2048,16]{1,2,0:T(8,128)}), f32[3,2048,16]{1,2,0:T(8,128)}) %all-reduce.9.cloned.1.call-update) | async-done | bytes 393232 | tf_op jit(solution)/shard_map/psum | solution.py:53
  905.4 23.6 %all_to_all.38 = f32[8,4,3,2048]{3,1,2,0:T(4,128)S(1)} all-to-all(f32[8,4,3,2048]{3,1,2,0:T(4,128)S(1)} %fusion.49), channel_id=1, replica_groups=mesh['det'=4,'obs'=8] {'obs'}, dimensions={0} | all-to-all | bytes 1572864 | tf_op jit(solution)/shard_map/all_to_all | solution.py:213
  932.2 23.6 %all_to_all.39 = f32[8,4,3,2048]{3,1,2,0:T(4,128)S(1)} all-to-all(f32[8,4,3,2048]{3,1,2,0:T(4,128)S(1)} %fusion.13), channel_id=1, replica_groups=mesh['det'=4,'obs'=8] {'obs'}, dimensions={0} | all-to-all | bytes 1572864 | tf_op jit(solution)/shard_map/all_to_all | solution.py:195
  962.1 57.2 %scatter_custom_fusion.2 = f32[40]{0:T(128)S(1)} fusion(s32[8192]{0:T(1024)} %convert_element_type.34, f32[8192]{0:T(1024)S(1)} %add_subtract_fusion, f32[]{:T(128)} %constant.148.clone.1), kind=kCustom, calls=%fused_computation.226 | custom fusion | flops 8192 | bytes 672 | tf_op jit(solution)/shard_map/scatter-add | solution.py:218
  1019.9 41.3 %psum.55 = f32[]{:T(128)} all-reduce(f32[]{:T(128)} %multiply_reduce_fusion), channel_id=1, replica_groups=mesh['det'=4,'obs'=8] {'det','obs'}, use_global_device_ids=true, to_apply=%region_18.21 | all-reduce | flops 1 | bytes 8 | tf_op jit(solution)/shard_map/psum | solution.py:224
  (188 shorter events, 106.0 us)
Async XLA Ops:
  7.2 7.1 copy-start.14
  7.2 65.7 %all-reduce.5.cloned.1.call-start = ((), (), s32[]{:S(2)}) async-start(), calls=%async_computation.7 | async-start | bytes 2359296 | tf_op jit(solution)/shard_map/psum | solution.py:53
  8.9 5.3 copy-start
  8.9 5.3 copy-start.2
  11.0 3.3 copy-start.5
  16.2 1.1 copy-start.17
  17.5 452.3 %copy-start.7 = (s32[16]{0:T(128)}, s32[16]{0:T(128)S(1)}, u32[]{:S(2)}) copy-start(s32[16]{0:T(128)S(1)} %fusion.103) | copy-start | bytes 196
  18.3 59.0 %all-to-all-start = ((s32[8,1,4]{2,1,0:T(1,128)}), s32[8,1,4]{2,1,0:T(1,128)S(1)}, u32[]{:S(2)}, u32[]{:S(2)}) async-start(s32[8,1,4]{2,1,0:T(1,128)} %bitcast.10), calls=%async_computation | async-start | bytes 8192 | tf_op jit(solution)/shard_map/all_to_all | solution.py:178
  77.3 5.9 copy-start.15
  77.3 57.0 %all-to-all-start.1 = ((f32[8,4,9,2048]{3,1,2,0:T(4,128)}), f32[8,4,9,2048]{3,1,2,0:T(4,128)S(1)}, u32[]{:S(2)}, u32[]{:S(2)}) async-start(f32[8,4,9,2048]{3,1,2,0:T(4,128)} %fusion.34), calls=%async_computation.1 | async-start | bytes 4718592 | tf_op jit(solution)/shard_map/all_to_all | solution.py:177
  142.9 320.9 %all-to-all-start.2 = ((f32[8,4,3,2048]{3,1,2,0:T(4,128)}), f32[8,4,3,2048]{3,1,2,0:T(4,128)}, u32[]{:S(2)}, u32[]{:S(2)}) async-start(f32[8,4,3,2048]{3,1,2,0:T(4,128)} %fusion.17), calls=%async_computation.2 | async-start | bytes 1572864 | tf_op jit(solution)/shard_map/all_to_all | solution.py:195
  150.5 465.4 %all-reduce.7.cloned.1.call-start = ((), (), s32[]{:S(2)}) async-start(), calls=%async_computation.8 | async-start | bytes 786432 | tf_op jit(solution)/shard_map/psum | solution.py:53
  463.8 12.8 %copy-start.10 = (s32[1024]{0:T(1024)}, s32[1024]{0:T(1024)S(1)}, u32[]{:S(2)}) copy-start(s32[1024]{0:T(1024)S(1)} %pad_clamp_fusion) | copy-start | bytes 12292
  463.8 14.5 %copy-start.11 = (pred[32]{0:T(512)(128)(4,1)}, pred[32]{0:T(512)(128)(4,1)S(1)}, u32[]{:S(2)}) copy-start(pred[32]{0:T(512)(128)(4,1)S(1)} %compare_and_fusion.1) | copy-start | bytes 100
  472.7 5.8 copy-start.6
  472.7 6.6 copy-start.1
  472.7 6.6 copy-start.3
  472.7 6.6 copy-start.4
  571.6 332.2 %all-reduce.9.cloned.1.call-start = ((), (), s32[]{:S(2)}) async-start(), calls=%async_computation.9 | async-start | bytes 786432 | tf_op jit(solution)/shard_map/psum | solution.py:53
  668.4 4.3 copy-start.8
  675.6 5.7 copy-start.12
  956.5 1.1 copy-start.9
  959.2 1.9 copy-start.13
  959.2 103.3 %copy-start.16 = (s32[1,1,40]{2,1,0:T(1,128)S(1)}, s32[1,1,40]{2,1,0:T(1,128)}, u32[]{:S(2)}) copy-start(s32[1,1,40]{2,1,0:T(1,128)} %param.16) | copy-start | bytes 484
Sparse Core Ops, SparseCore 0:
  17.4 55.4 all-reduce.4
  571.8 44.0 all-reduce.6
  860.0 43.8 all-reduce.8
where the time goes:
time: 1080 us; the launch traced here: 1070 us
  other arithmetic  534 us (49%)
  blocking collectives  217 us (20%)
  waiting for transfers between devices  187 us (17%)
  local copies, waits for them, and re-layouts  58.7 us (5%)
  matrix products  35.6 us (3%)
  between operations  19 us (2%)
  starting transfers between devices  18.9 us (2%)
    select_n x12, other arithmetic, body(): jnp.searchsorted(ends, jnp.arange(samples, dtype=jnp.int32), side='right')  300 us
    psum x3, waiting for transfers between devices, combine_det(): total = lax.psum(partial_value, 'det')  137 us
    scatter-add x2, other arithmetic, body(): jax.ops.segment_sum(expanded - unbin_local(apply_local_map), base_index,...  114 us
    psum x2, blocking collectives, squares(): return lax.psum(jnp.sum(residual_vector * residual_vector), ('det', 'obs'))  81.2 us
    scatter-add x1, other arithmetic, body(): jax.ops.segment_sum(cleaned, base_index, num_segments=nbase, indices_are_...  57.2 us
    mul x2, other arithmetic, body(): expanded * cos_w  51.5 us
    all_to_all x1, waiting for transfers between devices, body(): lax.all_to_all(pack_map(first_total), 'obs', split_axis=0, concat_axis=0,...  50 us
    all_to_all x2, blocking collectives, body(): lax.all_to_all(pack_map(apply_total), 'obs', split_axis=0, concat_axis=0,...  47.4 us
  transfers between devices with their start and end apart: 6, of which 4 were waited for; matrix products, arithmetic and copies ran while one was open for 30% of the time, Pallas kernels for 0%

commit v1 on v0

--- a/solution.py
+++ b/solution.py
@@ -50,7 +50,7 @@
 
 
 def combine_det(partial_value):
-    total = lax.psum(partial_value, "det")
+    total = jnp.sum(lax.all_gather(partial_value, "det"), axis=0)
     return total
 
 

time: 1080 us -> 1070 us (level)
  waiting for transfers between devices: 187 us -> 164 us
    psum x3 -> x0, waiting for transfers between devices: 137 us -> none  [combine_det(): total = lax.psum(partial_value, 'det')]
    all_gather x0 -> x3, waiting for transfers between devices: none -> 114 us  [combine_det(): total = jnp.sum(lax.all_gather(partial_value, 'det'), axis=0)]
    another operation x1 -> x7, local copies, waits for them, and re-layouts: 0.09 us -> 14 us  [the longest x6 13.9 us: combine_det(): total = jnp.sum(lax.all_gather(partial_value, 'det'), axis=0)]
where the time goes in v1:
time: 1070 us; the launch traced here: 1060 us
  other arithmetic  541 us (51%)
  blocking collectives  217 us (20%)
  waiting for transfers between devices  164 us (15%)
  local copies, waits for them, and re-layouts  62.9 us (6%)
  matrix products  34.3 us (3%)
  starting transfers between devices  18.6 us (2%)
  between operations  18.6 us (2%)
    select_n x12, other arithmetic, body(): jnp.searchsorted(ends, jnp.arange(samples, dtype=jnp.int32), side='right')  300 us
    scatter-add x2, other arithmetic, body(): jax.ops.segment_sum(expanded - unbin_local(apply_local_map), base_index,...  114 us
    all_gather x3, waiting for transfers between devices, combine_det(): total = jnp.sum(lax.all_gather(partial_value, 'det'), axis=0)  114 us
    psum x2, blocking collectives, squares(): return lax.psum(jnp.sum(residual_vector * residual_vector), ('det', 'obs'))  81.1 us
    scatter-add x1, other arithmetic, body(): jax.ops.segment_sum(cleaned, base_index, num_segments=nbase, indices_are_...  57 us
    mul x2, other arithmetic, body(): expanded * cos_w  52.2 us
    all_to_all x1, waiting for transfers between devices, body(): lax.all_to_all(pack_map(first_total), 'obs', split_axis=0, concat_axis=0,...  50 us
    all_to_all x2, blocking collectives, body(): lax.all_to_all(pack_map(apply_total), 'obs', split_axis=0, concat_axis=0,...  47.6 us
  transfers between devices with their start and end apart: 6, of which 4 were waited for; matrix products, arithmetic and copies ran while one was open for 30% of the time, Pallas kernels for 0%

profile of v1, /device:TPU:12, one launch (start us, length us, event | category | flops | bytes accessed | tf_op | source)
XLA Modules:
  0.0 1056.4 jit_solution(10929932766580426875)
XLA Ops:
  21.6 5.3 all-to-all-start
  27.1 51.8 %all-gather.4.cloned.1.call-done = f32[4,16,9,2048]{3,1,2,0:T(8,128)} async-done(((f32[1,16,9,2048]{3,1,2,0:T(8,128)}), f32[4,16,9,2048]{3,1,2,0:T(8,128)}) %all-gather.4.cloned.1.call-update) | async-done | bytes 4718608 | tf_op jit(solution)/shard_map/all_gather | solution.py:53
  84.8 5.5 all-to-all-start.1
  91.5 50.0 %all-to-all-done.1 = f32[8,4,9,2048]{3,1,2,0:T(4,128)S(1)} async-done(((f32[8,4,9,2048]{3,1,2,0:T(4,128)}), f32[8,4,9,2048]{3,1,2,0:T(4,128)S(1)}, u32[]{:S(2)}, u32[]{:S(2)}) %all-to-all-start.1) | async-done | bytes 2359328 | tf_op jit(solution)/shard_map/all_to_all | solution.py:177
  150.1 7.5 all-to-all-start.2
  157.9 312.6 %while.24 = (s32[]{:T(128)}, u32[8192]{0:T(1024)S(1)}, u32[8192]{0:T(1024)S(1)}, s32[40]{0:T(128)S(1)}, s32[]{:T(128)}, /*index=5*/s32[]{:T(128)}) while((s32[]{:T(128)}, u32[8192]{0:T(1024)S(1)}, u32[8192]{0:T(1024)S(1)}, s32[40]{0:T(128)S(1)}, s32[]{:T(128)}, /*index=5*/s32[]{:T(128)}) %tuple.233), condition=%wide.region_2.3_spmd.clone, body=%wide.region_1.2_spmd.clone.sunk | while | flops 1392643 | bytes 262864 | solution.py:80
  160.0 25.0 %fusion.150 = u32[8192]{0:T(1024)S(1)} fusion(u32[8192]{0:T(1024)S(1)} %get-tuple-element.525, u32[8192]{0:T(1024)S(1)} %get-tuple-element.524, s32[]{:T(128)} %bitcast.468, s32[]{:T(128)} %bitcast.469, s32[]{:T(128)} %bitcast.470, s32[]{:T(128)} %bitcast.471, s32[]{:T(128)} %bitcast.472, s32[]{:T(128)} %bitcast.473, s32[]{:T(128)} %bitcast.474, ...), kind=kLoop, calls=%fused_computation.8.clone.1 | loop fusion | flops 696320 | bytes 98465 | tf_op jit(solution)/shard_map/jit(searchsorted)/jit(_searchsorted_scan_impl)/vmap(jit(_searchsorted_scan_impl))/while/body/eval_jaxpr/select_n | solution.py:80
  185.0 25.0 %fusion.149 = u32[8192]{0:T(1024)S(1)} fusion(u32[8192]{0:T(1024)S(1)} %get-tuple-element.525, u32[8192]{0:T(1024)S(1)} %get-tuple-element.524, s32[]{:T(128)} %bitcast.468, s32[]{:T(128)} %bitcast.469, s32[]{:T(128)} %bitcast.470, s32[]{:T(128)} %bitcast.471, s32[]{:T(128)} %bitcast.472, s32[]{:T(128)} %bitcast.473, s32[]{:T(128)} %bitcast.474, ...), kind=kLoop, calls=%fused_computation.9.clone.1 | loop fusion | flops 696320 | bytes 98465 | tf_op jit(solution)/shard_map/jit(searchsorted)/jit(_searchsorted_scan_impl)/vmap(jit(_searchsorted_scan_impl))/while/body/eval_jaxpr/select_n | solution.py:80
  212.1 25.0 %fusion.150 = u32[8192]{0:T(1024)S(1)} fusion(u32[8192]{0:T(1024)S(1)} %get-tuple-element.525, u32[8192]{0:T(1024)S(1)} %get-tuple-element.524, s32[]{:T(128)} %bitcast.468, s32[]{:T(128)} %bitcast.469, s32[]{:T(128)} %bitcast.470, s32[]{:T(128)} %bitcast.471, s32[]{:T(128)} %bitcast.472, s32[]{:T(128)} %bitcast.473, s32[]{:T(128)} %bitcast.474, ...), kind=kLoop, calls=%fused_computation.8.clone.1 | loop fusion | flops 696320 | bytes 98465 | tf_op jit(solution)/shard_map/jit(searchsorted)/jit(_searchsorted_scan_impl)/vmap(jit(_searchsorted_scan_impl))/while/body/eval_jaxpr/select_n | solution.py:80
  237.1 25.0 %fusion.149 = u32[8192]{0:T(1024)S(1)} fusion(u32[8192]{0:T(1024)S(1)} %get-tuple-element.525, u32[8192]{0:T(1024)S(1)} %get-tuple-element.524, s32[]{:T(128)} %bitcast.468, s32[]{:T(128)} %bitcast.469, s32[]{:T(128)} %bitcast.470, s32[]{:T(128)} %bitcast.471, s32[]{:T(128)} %bitcast.472, s32[]{:T(128)} %bitcast.473, s32[]{:T(128)} %bitcast.474, ...), kind=kLoop, calls=%fused_computation.9.clone.1 | loop fusion | flops 696320 | bytes 98465 | tf_op jit(solution)/shard_map/jit(searchsorted)/jit(_searchsorted_scan_impl)/vmap(jit(_searchsorted_scan_impl))/while/body/eval_jaxpr/select_n | solution.py:80
  264.2 25.0 %fusion.150 = u32[8192]{0:T(1024)S(1)} fusion(u32[8192]{0:T(1024)S(1)} %get-tuple-element.525, u32[8192]{0:T(1024)S(1)} %get-tuple-element.524, s32[]{:T(128)} %bitcast.468, s32[]{:T(128)} %bitcast.469, s32[]{:T(128)} %bitcast.470, s32[]{:T(128)} %bitcast.471, s32[]{:T(128)} %bitcast.472, s32[]{:T(128)} %bitcast.473, s32[]{:T(128)} %bitcast.474, ...), kind=kLoop, calls=%fused_computation.8.clone.1 | loop fusion | flops 696320 | bytes 98465 | tf_op jit(solution)/shard_map/jit(searchsorted)/jit(_searchsorted_scan_impl)/vmap(jit(_searchsorted_scan_impl))/while/body/eval_jaxpr/select_n | solution.py:80
  289.2 25.0 %fusion.149 = u32[8192]{0:T(1024)S(1)} fusion(u32[8192]{0:T(1024)S(1)} %get-tuple-element.525, u32[8192]{0:T(1024)S(1)} %get-tuple-element.524, s32[]{:T(128)} %bitcast.468, s32[]{:T(128)} %bitcast.469, s32[]{:T(128)} %bitcast.470, s32[]{:T(128)} %bitcast.471, s32[]{:T(128)} %bitcast.472, s32[]{:T(128)} %bitcast.473, s32[]{:T(128)} %bitcast.474, ...), kind=kLoop, calls=%fused_computation.9.clone.1 | loop fusion | flops 696320 | bytes 98465 | tf_op jit(solution)/shard_map/jit(searchsorted)/jit(_searchsorted_scan_impl)/vmap(jit(_searchsorted_scan_impl))/while/body/eval_jaxpr/select_n | solution.py:80
  316.3 25.0 %fusion.150 = u32[8192]{0:T(1024)S(1)} fusion(u32[8192]{0:T(1024)S(1)} %get-tuple-element.525, u32[8192]{0:T(1024)S(1)} %get-tuple-element.524, s32[]{:T(128)} %bitcast.468, s32[]{:T(128)} %bitcast.469, s32[]{:T(128)} %bitcast.470, s32[]{:T(128)} %bitcast.471, s32[]{:T(128)} %bitcast.472, s32[]{:T(128)} %bitcast.473, s32[]{:T(128)} %bitcast.474, ...), kind=kLoop, calls=%fused_computation.8.clone.1 | loop fusion | flops 696320 | bytes 98465 | tf_op jit(solution)/shard_map/jit(searchsorted)/jit(_searchsorted_scan_impl)/vmap(jit(_searchsorted_scan_impl))/while/body/eval_jaxpr/select_n | solution.py:80
  341.3 25.0 %fusion.149 = u32[8192]{0:T(1024)S(1)} fusion(u32[8192]{0:T(1024)S(1)} %get-tuple-element.525, u32[8192]{0:T(1024)S(1)} %get-tuple-element.524, s32[]{:T(128)} %bitcast.468, s32[]{:T(128)} %bitcast.469, s32[]{:T(128)} %bitcast.470, s32[]{:T(128)} %bitcast.471, s32[]{:T(128)} %bitcast.472, s32[]{:T(128)} %bitcast.473, s32[]{:T(128)} %bitcast.474, ...), kind=kLoop, calls=%fused_computation.9.clone.1 | loop fusion | flops 696320 | bytes 98465 | tf_op jit(solution)/shard_map/jit(searchsorted)/jit(_searchsorted_scan_impl)/vmap(jit(_searchsorted_scan_impl))/while/body/eval_jaxpr/select_n | solution.py:80
  368.4 25.0 %fusion.150 = u32[8192]{0:T(1024)S(1)} fusion(u32[8192]{0:T(1024)S(1)} %get-tuple-element.525, u32[8192]{0:T(1024)S(1)} %get-tuple-element.524, s32[]{:T(128)} %bitcast.468, s32[]{:T(128)} %bitcast.469, s32[]{:T(128)} %bitcast.470, s32[]{:T(128)} %bitcast.471, s32[]{:T(128)} %bitcast.472, s32[]{:T(128)} %bitcast.473, s32[]{:T(128)} %bitcast.474, ...), kind=kLoop, calls=%fused_computation.8.clone.1 | loop fusion | flops 696320 | bytes 98465 | tf_op jit(solution)/shard_map/jit(searchsorted)/jit(_searchsorted_scan_impl)/vmap(jit(_searchsorted_scan_impl))/while/body/eval_jaxpr/select_n | solution.py:80
  393.4 25.0 %fusion.149 = u32[8192]{0:T(1024)S(1)} fusion(u32[8192]{0:T(1024)S(1)} %get-tuple-element.525, u32[8192]{0:T(1024)S(1)} %get-tuple-element.524, s32[]{:T(128)} %bitcast.468, s32[]{:T(128)} %bitcast.469, s32[]{:T(128)} %bitcast.470, s32[]{:T(128)} %bitcast.471, s32[]{:T(128)} %bitcast.472, s32[]{:T(128)} %bitcast.473, s32[]{:T(128)} %bitcast.474, ...), kind=kLoop, calls=%fused_computation.9.clone.1 | loop fusion | flops 696320 | bytes 98465 | tf_op jit(solution)/shard_map/jit(searchsorted)/jit(_searchsorted_scan_impl)/vmap(jit(_searchsorted_scan_impl))/while/body/eval_jaxpr/select_n | solution.py:80
  420.5 25.0 %fusion.150 = u32[8192]{0:T(1024)S(1)} fusion(u32[8192]{0:T(1024)S(1)} %get-tuple-element.525, u32[8192]{0:T(1024)S(1)} %get-tuple-element.524, s32[]{:T(128)} %bitcast.468, s32[]{:T(128)} %bitcast.469, s32[]{:T(128)} %bitcast.470, s32[]{:T(128)} %bitcast.471, s32[]{:T(128)} %bitcast.472, s32[]{:T(128)} %bitcast.473, s32[]{:T(128)} %bitcast.474, ...), kind=kLoop, calls=%fused_computation.8.clone.1 | loop fusion | flops 696320 | bytes 98465 | tf_op jit(solution)/shard_map/jit(searchsorted)/jit(_searchsorted_scan_impl)/vmap(jit(_searchsorted_scan_impl))/while/body/eval_jaxpr/select_n | solution.py:80
  445.5 25.0 %fusion.149 = u32[8192]{0:T(1024)S(1)} fusion(u32[8192]{0:T(1024)S(1)} %get-tuple-element.525, u32[8192]{0:T(1024)S(1)} %get-tuple-element.524, s32[]{:T(128)} %bitcast.468, s32[]{:T(128)} %bitcast.469, s32[]{:T(128)} %bitcast.470, s32[]{:T(128)} %bitcast.471, s32[]{:T(128)} %bitcast.472, s32[]{:T(128)} %bitcast.473, s32[]{:T(128)} %bitcast.474, ...), kind=kLoop, calls=%fused_computation.9.clone.1 | loop fusion | flops 696320 | bytes 98465 | tf_op jit(solution)/shard_map/jit(searchsorted)/jit(_searchsorted_scan_impl)/vmap(jit(_searchsorted_scan_impl))/while/body/eval_jaxpr/select_n | solution.py:80
  486.1 57.0 %scatter_custom_fusion = f32[40]{0:T(128)S(1)} fusion(s32[8192]{0:T(1024)S(1)} %convert_element_type.34, f32[8192]{0:T(1024)S(1)} %add_subtract_fusion.2, f32[]{:T(128)} %constant.148.clone.1), kind=kCustom, calls=%fused_computation.230 | custom fusion | flops 8192 | bytes 164 | tf_op jit(solution)/shard_map/scatter-add | solution.py:202
  545.1 26.0 %fusion.114 = (f32[8192]{0:T(1024)S(1)}, f32[8192]{0:T(1024)S(1)}, pred[8192]{0:T(1024)(128)(4,1)S(1)}, pred[8192]{0:T(1024)(128)(4,1)S(1)}, pred[8192]{0:T(1024...) fusion(f32[8192]{0:T(1024)S(1)} %bitcast.527, ...), kind=kLoop, calls=%fused_computation.235 | loop fusion | flops 712704 | bytes 458912 | tf_op jit(solution)/shard_map/mul | solution.py:211
  578.9 30.9 %all-gather.6.cloned.1.call-done = f32[4,16,3,2048]{3,1,2,0:T(8,128)} async-done(((f32[1,16,3,2048]{3,1,2,0:T(8,128)}), f32[4,16,3,2048]{3,1,2,0:T(8,128)}) %all-gather.6.cloned.1.call-update) | async-done | bytes 1572880 | tf_op jit(solution)/shard_map/all_gather | solution.py:53
  613.7 24.0 %all_to_all.36 = f32[8,4,3,2048]{3,1,2,0:T(4,128)S(1)} all-to-all(f32[8,4,3,2048]{3,1,2,0:T(4,128)S(1)} %fusion.51), channel_id=1, replica_groups=mesh['det'=4,'obs'=8] {'obs'}, dimensions={0} | all-to-all | bytes 1572864 | tf_op jit(solution)/shard_map/all_to_all | solution.py:213
  641.0 23.4 %all_to_all.37 = f32[8,4,3,2048]{3,1,2,0:T(4,128)S(1)} all-to-all(f32[8,4,3,2048]{3,1,2,0:T(4,128)S(1)} %fusion.15), channel_id=1, replica_groups=mesh['det'=4,'obs'=8] {'obs'}, dimensions={0} | all-to-all | bytes 1572864 | tf_op jit(solution)/shard_map/all_to_all | solution.py:195
  678.9 57.2 %scatter_custom_fusion.1 = f32[40]{0:T(128)S(1)} fusion(s32[8192]{0:T(1024)} %copy-done.1, f32[8192]{0:T(1024)S(1)} %add_subtract_fusion.1, f32[]{:T(128)} %constant.148.clone.1), kind=kCustom, calls=%fused_computation.228 | custom fusion | flops 8192 | bytes 672 | tf_op jit(solution)/shard_map/scatter-add | solution.py:218
  736.6 41.2 %all-reduce = (f32[]{:T(128)}, f32[]{:T(128)}) all-reduce(f32[]{:T(128)} %get-tuple-element.196, f32[]{:T(128)} %get-tuple-element.195), channel_id=1, replica_groups=mesh['det'=4,'obs'=8] {'det','obs'}, use_global_device_ids=true, to_apply=%region_8.10 | all-reduce | flops 2 | bytes 16 | tf_op jit(solution)/shard_map/psum | solution.py:58
  779.8 39.9 %psum.30 = f32[]{:T(128)} all-reduce(f32[]{:T(128)} %get-tuple-element.209), channel_id=1, replica_groups=mesh['det'=4,'obs'=8] {'det','obs'}, use_global_device_ids=true, to_apply=%region_14.17 | all-reduce | flops 1 | bytes 8 | tf_op jit(solution)/shard_map/psum | solution.py:58
  823.1 26.2 %fusion.113 = (f32[8192]{0:T(1024)S(1)}, f32[8192]{0:T(1024)S(1)}) fusion(f32[8192]{0:T(1024)S(1)} %bitcast.529, pred[8192]{0:T(1024)(128)(4,1)} %get-tuple-element.252, pred[8192]{0:T(1024)(128)(4,1)} %get-tuple-element.251, pred[8192]{0:T(1024)(128)(4,1)} %get-tuple-element.250, pred[8192]{0:T(1024)(128)(4,1)} %get-tuple-element.249, ...), kind=kLoop, calls=%fused_computation.234 | loop fusion | flops 335872 | bytes 426144 | tf_op jit(solution)/shard_map/mul | solution.py:211
  857.0 30.8 %all-gather.8.cloned.1.call-done = f32[4,16,3,2048]{3,1,2,0:T(8,128)} async-done(((f32[1,16,3,2048]{3,1,2,0:T(8,128)}), f32[4,16,3,2048]{3,1,2,0:T(8,128)}) %all-gather.8.cloned.1.call-update) | async-done | bytes 1572880 | tf_op jit(solution)/shard_map/all_gather | solution.py:53
  891.6 23.6 %all_to_all.38 = f32[8,4,3,2048]{3,1,2,0:T(4,128)S(1)} all-to-all(f32[8,4,3,2048]{3,1,2,0:T(4,128)S(1)} %fusion.49), channel_id=1, replica_groups=mesh['det'=4,'obs'=8] {'obs'}, dimensions={0} | all-to-all | bytes 1572864 | tf_op jit(solution)/shard_map/all_to_all | solution.py:213
  918.5 23.6 %all_to_all.39 = f32[8,4,3,2048]{3,1,2,0:T(4,128)S(1)} all-to-all(f32[8,4,3,2048]{3,1,2,0:T(4,128)S(1)} %fusion.13), channel_id=1, replica_groups=mesh['det'=4,'obs'=8] {'obs'}, dimensions={0} | all-to-all | bytes 1572864 | tf_op jit(solution)/shard_map/all_to_all | solution.py:195
  948.3 57.2 %scatter_custom_fusion.2 = f32[40]{0:T(128)S(1)} fusion(s32[8192]{0:T(1024)} %copy-done.1, f32[8192]{0:T(1024)S(1)} %add_subtract_fusion, f32[]{:T(128)} %constant.148.clone.1), kind=kCustom, calls=%fused_computation.226 | custom fusion | flops 8192 | bytes 672 | tf_op jit(solution)/shard_map/scatter-add | solution.py:218
  1006.0 41.2 %psum.31 = f32[]{:T(128)} all-reduce(f32[]{:T(128)} %multiply_reduce_fusion), channel_id=1, replica_groups=mesh['det'=4,'obs'=8] {'det','obs'}, use_global_device_ids=true, to_apply=%region_18.21 | all-reduce | flops 1 | bytes 8 | tf_op jit(solution)/shard_map/psum | solution.py:224
  (181 shorter events, 115.7 us)
Async XLA Ops:
  7.2 7.0 copy-start.9
  7.2 71.7 %all-gather.4.cloned.1.call-start = ((), (), s32[]{:S(2)}) async-start(), calls=%async_computation.7 | async-start | bytes 5898240 | tf_op jit(solution)/shard_map/all_gather | solution.py:53
  17.3 3.4 copy-start.12
  20.9 455.7 %copy-start.2 = (s32[16]{0:T(128)}, s32[16]{0:T(128)S(1)}, u32[]{:S(2)}) copy-start(s32[16]{0:T(128)S(1)} %fusion.103) | copy-start | bytes 196
  21.6 63.2 %all-to-all-start = ((s32[8,1,4]{2,1,0:T(1,128)}), s32[8,1,4]{2,1,0:T(1,128)S(1)}, u32[]{:S(2)}, u32[]{:S(2)}) async-start(s32[8,1,4]{2,1,0:T(1,128)} %bitcast.10), calls=%async_computation | async-start | bytes 8192 | tf_op jit(solution)/shard_map/all_to_all | solution.py:178
  84.8 5.5 copy-start.10
  84.8 56.7 %all-to-all-start.1 = ((f32[8,4,9,2048]{3,1,2,0:T(4,128)}), f32[8,4,9,2048]{3,1,2,0:T(4,128)S(1)}, u32[]{:S(2)}, u32[]{:S(2)}) async-start(f32[8,4,9,2048]{3,1,2,0:T(4,128)} %fusion.34), calls=%async_computation.1 | async-start | bytes 4718592 | tf_op jit(solution)/shard_map/all_to_all | solution.py:177
  150.1 320.5 %all-to-all-start.2 = ((f32[8,4,3,2048]{3,1,2,0:T(4,128)}), f32[8,4,3,2048]{3,1,2,0:T(4,128)}, u32[]{:S(2)}, u32[]{:S(2)}) async-start(f32[8,4,3,2048]{3,1,2,0:T(4,128)} %fusion.17), calls=%async_computation.2 | async-start | bytes 1572864 | tf_op jit(solution)/shard_map/all_to_all | solution.py:195
  157.7 452.2 %all-gather.6.cloned.1.call-start = ((), (), s32[]{:S(2)}) async-start(), calls=%async_computation.8 | async-start | bytes 1966080 | tf_op jit(solution)/shard_map/all_gather | solution.py:53
  470.5 15.6 %copy-start.1 = (s32[8192]{0:T(1024)}, s32[8192]{0:T(1024)S(1)}, u32[]{:S(2)}) copy-start(s32[8192]{0:T(1024)S(1)} %convert_element_type.34) | copy-start | bytes 98308
  470.6 12.8 %copy-start.5 = (s32[1024]{0:T(1024)}, s32[1024]{0:T(1024)S(1)}, u32[]{:S(2)}) copy-start(s32[1024]{0:T(1024)S(1)} %pad_clamp_fusion) | copy-start | bytes 12292
  470.6 14.5 %copy-start.6 = (pred[32]{0:T(512)(128)(4,1)}, pred[32]{0:T(512)(128)(4,1)S(1)}, u32[]{:S(2)}) copy-start(pred[32]{0:T(512)(128)(4,1)S(1)} %compare_and_fusion.1) | copy-start | bytes 100
  481.0 5.1 copy-start
  578.9 308.9 %all-gather.8.cloned.1.call-start = ((), (), s32[]{:S(2)}) async-start(), calls=%async_computation.9 | async-start | bytes 1966080 | tf_op jit(solution)/shard_map/all_gather | solution.py:53
  666.3 2.9 copy-start.3
  672.1 5.7 copy-start.7
  943.1 0.6 copy-start.4
  945.4 1.9 copy-start.8
  945.9 102.6 %copy-start.11 = (s32[1,1,40]{2,1,0:T(1,128)S(1)}, s32[1,1,40]{2,1,0:T(1,128)}, u32[]{:S(2)}) copy-start(s32[1,1,40]{2,1,0:T(1,128)} %param.16) | copy-start | bytes 484
Sparse Core Ops, SparseCore 0:
  20.8 58.0 all-gather.3
  579.0 30.8 all-gather.5
  857.1 30.6 all-gather.7
